TPU v7x, 512 devices: a whole 4x8x8 slice. The times are simulated.
512 devices in a mesh: seq: 32 (over x, y), grp: 16 (over z, core).
Axes of the slice: x: 4, y: 8, z: 8, core: 2. Of those that a mesh axis runs over, the one named last changes fastest.
Arguments:
- normed_hidden_input: bfloat16 [65536, 4096], P(('grp', 'seq')), may hold values from -6 to 6
- frozen_query_rows: bfloat16 [65536, 4096], P(('grp', 'seq')), may hold values from -16 to 16
- frozen_key_rows: bfloat16 [65536, 1024], P(('grp', 'seq')), may hold values from -16 to 16
- attention_output_gradient: bfloat16 [65536, 4096], P(('grp', 'seq')), may hold values from -0.15625 to 0.15625
- adapter_down_weight: bfloat16 [256, 64, 4096], P('grp', None, 'seq'), may hold values from -0.09375 to 0.09375
- adapter_up_weight: bfloat16 [256, 64, 1024], P('grp', 'seq'), may hold values from -0.75 to 0.75
- segment_adapter_index: int32 [16, 16], replicated, may hold values from 0 to 255, as said below
- segment_block_count: int32 [16, 16], replicated, may hold values from 1 to 16, 32 in all within a row
- adapter_row_index: int32 [256], replicated, may hold values from 0 to 255, as said below
Outputs:
- down_grad: float32 [256, 64, 4096], P('grp', None, 'seq')
- up_grad: float32 [256, 64, 1024], P('grp', 'seq')
Inputs may be any that keep to these rules, and one draw needn't show every extreme that they name: A permutation: adapter a is held in row adapter_row_index[a] of adapter_down_weight and adapter_up_weight. `segment_adapter_index`: call rows g * 16 to (g + 1) * 16 - 1 of adapter_down_weight the rows of index g of grp. In each sequence at most 2 segments use adapters held in the rows of one index of grp, and in every sequence some index holds exactly 2 of them. Tenants may repeat within and across sequences. `segment_block_count`: each row sums to 32; in each row some segment has exactly 16 blocks.
All inputs are finite; a program needn't handle non-finite values.
Results may differ from a plain program's by a relative error of at most 0.0056.
Values may be sent and summed in bfloat16 or wider, within the bound.
No kernel may reach another device: no remote copies, remote signals or barrier semaphores. Data moves between devices by JAX's collectives and lax.ppermute only.
A program may use at most 64 MiB of HBM per device.

v0:
```python
import math
import jax
import jax.numpy as jnp
from jax import lax
from jax.sharding import PartitionSpec as P

HEAD_DIM = 128
BLOCK = 128
QROWS = 512
adapter_scale = 2.0


def attend_head(query_head, key_head, grad_head, segment_ids, query_rows, reach):
    length, head_width = query_head.shape
    padded_keys = jnp.concatenate([jnp.zeros((reach, head_width), key_head.dtype), key_head], 0)
    padded_ids = jnp.concatenate([jnp.full((reach,), -1, jnp.int32), segment_ids], 0)
    window = query_rows + reach
    factor = 1.0 / math.sqrt(head_width)

    def one_block(totals, number):
        offset = number * query_rows
        query_block = lax.dynamic_slice_in_dim(query_head, offset, query_rows, 0)
        grad_block = lax.dynamic_slice_in_dim(grad_head, offset, query_rows, 0)
        key_block = lax.dynamic_slice_in_dim(padded_keys, offset, window, 0)
        key_ids = lax.dynamic_slice_in_dim(padded_ids, offset, window, 0)
        query_ids = lax.dynamic_slice_in_dim(segment_ids, offset, query_rows, 0)
        scores = jnp.dot(query_block, key_block.T, preferred_element_type=jnp.float32) * factor
        query_pos = offset + jnp.arange(query_rows, dtype=jnp.int32)
        key_pos = offset - reach + jnp.arange(window, dtype=jnp.int32)
        allowed = (key_ids[None, :] == query_ids[:, None]) & (
            key_pos[None, :] <= query_pos[:, None]
        )
        scores = jnp.where(allowed, scores, jnp.float32(-1e30))
        highest = jnp.max(scores, axis=1, keepdims=True)
        expo = jnp.exp(scores - highest)
        probabilities = (expo / jnp.sum(expo, axis=1, keepdims=True)).astype(jnp.bfloat16)
        contribution = jnp.dot(probabilities.T, grad_block, preferred_element_type=jnp.float32)
        current = lax.dynamic_slice_in_dim(totals, offset, window, 0)
        totals = lax.dynamic_update_slice_in_dim(totals, current + contribution, offset, 0)
        return (totals, None)

    initial = jnp.zeros((length + reach, head_width), jnp.float32)
    totals, _ = lax.scan(one_block, initial, jnp.arange(length // query_rows, dtype=jnp.int32))
    return totals[reach:].astype(jnp.bfloat16)


def local(
    normed_hidden_input,
    frozen_query_rows,
    frozen_key_rows,
    attention_output_gradient,
    adapter_down_weight,
    adapter_up_weight,
    segment_adapter_index,
    segment_block_count,
    adapter_row_index,
):
    group_count = lax.axis_size("grp")
    shard_count = lax.axis_size("seq")
    group_index = lax.axis_index("grp")
    tokens_here, model_width = normed_hidden_input.shape
    portion_width = adapter_down_weight.shape[2]
    resident_adapters, rank_overall = (adapter_down_weight.shape[0], adapter_down_weight.shape[1])
    rank_portion, value_projection_width = (adapter_up_weight.shape[1], adapter_up_weight.shape[2])
    segments = segment_adapter_index.shape[1]
    capacity = max(2, (segments + group_count - 1) // group_count)
    seq_length = tokens_here * shard_count
    block_total = seq_length // BLOCK
    block_here = tokens_here // BLOCK
    reach = min(16, seq_length // (2 * BLOCK)) * BLOCK
    head_total = frozen_query_rows.shape[1] // HEAD_DIM
    kv_heads = value_projection_width // HEAD_DIM
    heads_here = head_total // shard_count
    group_size = head_total // kv_heads
    slot_total = group_count * capacity
    adapter_ids = jnp.arange(adapter_row_index.shape[0], dtype=jnp.int32)
    slot_of = jnp.sum(
        jnp.where(segment_adapter_index[:, :, None] == adapter_ids, adapter_row_index, 0), axis=2
    )
    owner_group = slot_of // resident_adapters
    local_slot = slot_of % resident_adapters
    order_ids = jnp.arange(segments, dtype=jnp.int32)
    earlier = order_ids[:, None] > order_ids[None, :]
    same_owner = owner_group[:, :, None] == owner_group[:, None, :]
    rank_in_owner = jnp.sum((same_owner & earlier[None]).astype(jnp.int32), axis=2)
    placement = owner_group * capacity + rank_in_owner
    capacity_ids = jnp.arange(capacity, dtype=jnp.int32)
    local_ids = jnp.arange(resident_adapters, dtype=jnp.int32)
    picks = (
        (owner_group == group_index)[:, :, None, None]
        & (rank_in_owner[:, :, None, None] == capacity_ids[:, None])
        & (local_slot[:, :, None, None] == local_ids)
    )
    chooser = jnp.sum(picks.astype(jnp.float32), axis=1)
    selector_half = chooser.astype(jnp.bfloat16)
    send_down = jnp.einsum(
        "pgl,lut->pgut", selector_half, adapter_down_weight, preferred_element_type=jnp.float32
    ).astype(jnp.bfloat16)
    send_up = jnp.einsum(
        "gyv,vmf->gymf", selector_half, adapter_up_weight, preferred_element_type=jnp.float32
    ).astype(jnp.bfloat16)
    fetched_down, fetched_up = (
        lax.all_to_all(send_down, "grp", split_axis=0, concat_axis=0, tiled=True),
        lax.all_to_all(send_up, "grp", split_axis=0, concat_axis=0, tiled=True),
    )
    own_blocks = segment_block_count[group_index]
    ends = jnp.cumsum(own_blocks)
    block_seg = jnp.sum(
        (jnp.arange(block_total, dtype=jnp.int32)[:, None] >= ends[None, :]).astype(jnp.int32),
        axis=1,
    )
    own_place = placement[group_index]
    block_place = jnp.sum(
        jnp.where(block_seg[:, None] == order_ids[None, :], own_place[None, :], 0), axis=1
    )
    block_pick = block_place[:, None] == jnp.arange(slot_total, dtype=jnp.int32)[None, :]
    pick_half = block_pick.astype(jnp.bfloat16)
    segment_ids = jnp.broadcast_to(block_seg[:, None], (block_total, BLOCK)).reshape(seq_length)
    block_down_weight = jnp.einsum(
        "bn,nrd->brd",
        pick_half,
        fetched_down.reshape(slot_total, rank_overall, portion_width),
        preferred_element_type=jnp.float32,
    ).astype(jnp.bfloat16)
    block_up_rows = jnp.einsum(
        "bn,nre->bre",
        pick_half,
        fetched_up.reshape(slot_total, rank_portion, value_projection_width),
        preferred_element_type=jnp.float32,
    ).astype(jnp.bfloat16)
    features = lax.all_to_all(normed_hidden_input, "seq", split_axis=1, concat_axis=0, tiled=True)
    amount = lax.axis_size("seq") * tokens_here
    token_rows = features.reshape(amount // BLOCK, BLOCK, portion_width)
    reduced_rank_part = (
        lax.psum_scatter(
            jnp.einsum(
                "jyw,jaw->jya", token_rows, block_down_weight, preferred_element_type=jnp.float32
            ).reshape(amount, rank_overall),
            "seq",
            scatter_dimension=0,
            tiled=True,
        )
        .astype(jnp.bfloat16)
        .reshape(block_here, BLOCK, rank_overall)
    )
    near_up = lax.all_to_all(block_up_rows, "seq", split_axis=0, concat_axis=1, tiled=True)
    query_grid = frozen_query_rows.reshape(tokens_here, shard_count, heads_here, HEAD_DIM)
    key_grid = jnp.repeat(
        frozen_key_rows.reshape(tokens_here, kv_heads, HEAD_DIM), group_size, axis=1
    ).reshape(tokens_here, shard_count, heads_here, HEAD_DIM)
    grad_grid = attention_output_gradient.reshape(tokens_here, shard_count, heads_here, HEAD_DIM)
    query_all = lax.all_to_all(query_grid, "seq", split_axis=1, concat_axis=0, tiled=True)
    key_all = lax.all_to_all(key_grid, "seq", split_axis=1, concat_axis=0, tiled=True)
    grad_all = lax.all_to_all(grad_grid, "seq", split_axis=1, concat_axis=0, tiled=True)

    def per_head(triple):
        return attend_head(triple[0], triple[1], triple[2], segment_ids, QROWS, reach)

    stacked = (
        jnp.moveaxis(query_all[:, 0], 1, 0),
        jnp.moveaxis(key_all[:, 0], 1, 0),
        jnp.moveaxis(grad_all[:, 0], 1, 0),
    )
    result = lax.map(per_head, stacked)
    head_grads = jnp.moveaxis(result, 0, 1)[:, None]
    token_grads = lax.all_to_all(head_grads, "seq", split_axis=0, concat_axis=1, tiled=True)
    value_grad = jnp.sum(
        token_grads.reshape(tokens_here, kv_heads, group_size, HEAD_DIM), axis=2, dtype=jnp.float32
    )
    value_row_blocks = value_grad.reshape(block_here, BLOCK, value_projection_width).astype(
        jnp.bfloat16
    )
    up_weight_terms = adapter_scale * jnp.einsum(
        "fvg,fvn->fgn", reduced_rank_part, value_row_blocks, preferred_element_type=jnp.float32
    )
    backward_rank_part = (
        adapter_scale
        * jnp.einsum("vaw,vpw->vap", value_row_blocks, near_up, preferred_element_type=jnp.float32)
    ).astype(jnp.bfloat16)
    all_low = lax.all_gather(
        backward_rank_part.reshape(tokens_here, rank_overall), "seq", axis=0, tiled=True
    )
    back_down = jnp.einsum(
        "jcy,jct->jyt",
        all_low.reshape(block_total, BLOCK, rank_overall),
        features.reshape(block_total, BLOCK, portion_width),
        preferred_element_type=jnp.float32,
    )
    back_up = lax.all_to_all(up_weight_terms, "seq", split_axis=1, concat_axis=0, tiled=True)
    pick_full = block_pick.astype(jnp.float32)
    slot_down = jnp.einsum("bn,brd->nrd", pick_full, back_down, precision=lax.Precision.HIGHEST)
    slot_up = jnp.einsum("bn,bre->nre", pick_full, back_up, precision=lax.Precision.HIGHEST)
    return_down, return_up = (
        lax.all_to_all(
            slot_down.reshape(group_count, capacity, rank_overall, portion_width),
            "grp",
            split_axis=0,
            concat_axis=0,
            tiled=True,
        ),
        lax.all_to_all(
            slot_up.reshape(group_count, capacity, rank_portion, value_projection_width),
            "grp",
            split_axis=0,
            concat_axis=0,
            tiled=True,
        ),
    )
    down_grad = jnp.einsum("nca,ncrd->ard", chooser, return_down, precision=lax.Precision.HIGHEST)
    up_grad = jnp.einsum("nca,ncre->are", chooser, return_up, precision=lax.Precision.HIGHEST)
    return (down_grad, up_grad)


def solution(mesh):
    return jax.shard_map(
        local,
        mesh=mesh,
        in_specs=(
            P(("grp", "seq"), None),
            P(("grp", "seq"), None),
            P(("grp", "seq"), None),
            P(("grp", "seq"), None),
            P("grp", None, "seq"),
            P("grp", "seq", None),
            P(),
            P(),
            P(),
        ),
        out_specs=(P("grp", None, "seq"), P("grp", "seq", None)),
        check_vma=False,
    )
```

profile of v0, /device:TPU:1, one launch (start us, length us, event | category | flops | bytes accessed | tf_op | source)
XLA Modules:
  0.0 591.7 jit_solution(1120349917430718640)
XLA Ops:
  11.0 11.8 %all-to-all-start.4 = ((bf16[16,2,2,1024]{3,2,1,0:T(2,128)(2,1)}), bf16[16,2,2,1024]{3,2,1,0:T(2,128)(2,1)S(1)}, u32[]{:S(2)}, u32[]{:S(2)}) async-start(bf16[16,2,2,1024]{3,2,1,0:T(2,128)(2,1)} %copy.109), calls=%async_computation.4 | async-start | bytes 262144 | tf_op jit(solution)/shard_map/all_to_all | solution.py:104
  25.0 7.0 %all-to-all-done.4 = bf16[16,2,2,1024]{3,2,1,0:T(2,128)(2,1)S(1)} async-done(((bf16[16,2,2,1024]{3,2,1,0:T(2,128)(2,1)}), bf16[16,2,2,1024]{3,2,1,0:T(2,128)(2,1)S(1)}, u32[]{:S(2)}, u32[]{:S(2)}) %all-to-all-start.4) | async-done | bytes 131104 | tf_op jit(solution)/shard_map/all_to_all | solution.py:104
  32.0 3.5 all-to-all-start.8
  35.5 16.8 %all-to-all-done.8 = bf16[16,2,64,128]{3,2,1,0:T(8,128)(2,1)S(1)} async-done(((bf16[16,2,64,128]{3,2,1,0:T(8,128)(2,1)}), bf16[16,2,64,128]{3,2,1,0:T(8,128)(2,1)S(1)}, u32[]{:S(2)}, u32[]{:S(2)}) %all-to-all-start.8) | async-done | bytes 524320 | tf_op jit(solution)/shard_map/all_to_all | solution.py:103
  53.5 9.7 %all-to-all-start.1 = ((bf16[128,32,1,128]{3,0,2,1:T(8,128)(2,1)}), bf16[128,32,1,128]{3,0,2,1:T(8,128)(2,1)S(1)}, u32[]{:S(2)}, u32[]{:S(2)}) async-start(bf16[128,32,1,128]{3,0,2,1:T(8,128)(2,1)} %bitcast.10), calls=%async_computation.1 | async-start | bytes 2097152 | tf_op jit(solution)/shard_map/all_to_all | solution.py:153
  66.2 25.2 %all-to-all-done.1 = bf16[128,32,1,128]{3,0,2,1:T(8,128)(2,1)S(1)} async-done(((bf16[128,32,1,128]{3,0,2,1:T(8,128)(2,1)}), bf16[128,32,1,128]{3,0,2,1:T(8,128)(2,1)S(1)}, u32[]{:S(2)}, u32[]{:S(2)}) %all-to-all-start.1) | async-done | bytes 1048608 | tf_op jit(solution)/shard_map/all_to_all | solution.py:153
  91.4 5.6 all-to-all-start.2
  99.9 22.2 %all-to-all-done.2 = bf16[128,32,1,128]{3,0,2,1:T(8,128)(2,1)} async-done(((bf16[128,32,1,128]{3,0,2,1:T(8,128)(2,1)}), bf16[128,32,1,128]{3,0,2,1:T(8,128)(2,1)}, u32[]{:S(2)}, u32[]{:S(2)}) %all-to-all-start.2) | async-done | bytes 1048608 | tf_op jit(solution)/shard_map/all_to_all | solution.py:154
  122.2 8.1 %all-to-all-start = ((bf16[128,32,1,128]{3,0,2,1:T(8,128)(2,1)}), bf16[128,32,1,128]{3,0,2,1:T(8,128)(2,1)}, u32[]{:S(2)}, u32[]{:S(2)}) async-start(bf16[128,32,1,128]{3,0,2,1:T(8,128)(2,1)} %copy.101), calls=%async_computation | async-start | bytes 2097152 | tf_op jit(solution)/shard_map/all_to_all | solution.py:152
  135.8 19.1 %all-to-all-done = bf16[128,32,1,128]{3,0,2,1:T(8,128)(2,1)} async-done(((bf16[128,32,1,128]{3,0,2,1:T(8,128)(2,1)}), bf16[128,32,1,128]{3,0,2,1:T(8,128)(2,1)}, u32[]{:S(2)}, u32[]{:S(2)}) %all-to-all-start) | async-done | bytes 1048608 | tf_op jit(solution)/shard_map/all_to_all | solution.py:152
  154.9 8.6 %all-to-all-start.6 = ((bf16[128,32,128]{2,0,1:T(8,128)(2,1)}), bf16[128,32,128]{2,0,1:T(8,128)(2,1)S(1)}, u32[]{:S(2)}, u32[]{:S(2)}) async-start(bf16[128,32,128]{2,0,1:T(8,128)(2,1)} %copy.113), calls=%async_computation.6 | async-start | bytes 2097152 | tf_op jit(solution)/shard_map/all_to_all | solution.py:131
  165.3 67.9 %while.19 = (s32[]{:T(128)}, f32[6144,128]{1,0:T(8,128)}, s32[8]{0:T(128)S(1)}, s32[6144]{0:T(1024)S(1)}, s32[4096]{0:T(1024)S(1)}, /*index=5*/bf16[4096,128]{1,...) while((s32[]{:T(128)}, f32[6144,128]{1,0:T(8,128)}, ...), condition=%wide.region_9.10_spmd, body=%wide.region_6.9_spmd.sunk | while | flops 685836288 | bytes 19343620 | solution.py:43
  170.0 3.8 fusion.64
  178.5 3.8 fusion.64
  187.0 3.8 fusion.64
  195.5 3.8 fusion.64
  204.0 3.8 fusion.64
  209.2 2.4 fusion.62
  212.5 3.8 fusion.64
  221.0 3.8 fusion.64
  229.5 3.8 fusion.64
  238.1 9.2 %all-to-all-start.3 = ((bf16[32,2,8192]{2,1,0:T(2,128)(2,1)}), bf16[32,2,8192]{2,1,0:T(2,128)(2,1)S(1)}, u32[]{:S(2)}, u32[]{:S(2)}) async-start(bf16[32,2,8192]{2,1,0:T(2,128)(2,1)} %reshape.260), calls=%async_computation.3 | async-start | bytes 2097152 | tf_op jit(solution)/shard_map/all_to_all | solution.py:166
  251.6 20.3 %all-to-all-done.3 = bf16[32,2,8192]{2,1,0:T(2,128)(2,1)S(1)} async-done(((bf16[32,2,8192]{2,1,0:T(2,128)(2,1)}), bf16[32,2,8192]{2,1,0:T(2,128)(2,1)S(1)}, u32[]{:S(2)}, u32[]{:S(2)}) %all-to-all-start.3) | async-done | bytes 1048608 | tf_op jit(solution)/shard_map/all_to_all | solution.py:166
  272.9 8.3 %all-to-all-start.5 = ((bf16[32,2,1024]{2,1,0:T(2,128)(2,1)}), bf16[32,2,1024]{2,1,0:T(2,128)(2,1)S(1)}, u32[]{:S(2)}, u32[]{:S(2)}) async-start(bf16[32,2,1024]{2,1,0:T(2,128)(2,1)} %copy.111), calls=%async_computation.5 | async-start | bytes 262144 | tf_op jit(solution)/shard_map/all_to_all | solution.py:146
  281.3 4.3 reshape.261
  288.3 176.5 %reduce-scatter.2.cloned.1.call-done = f32[128,64]{0,1:T(8,128)} async-done(((f32[4096,64]{0,1:T(8,128)}), f32[128,64]{0,1:T(8,128)}) %reduce-scatter.2.cloned.1.call-update) | async-done | bytes 32784 | tf_op jit(solution)/shard_map/reduce_scatter | solution.py:135
  466.8 6.5 %all-to-all-start.9 = ((f32[1,64,1024]{2,0,1:T(1,128)}), f32[1,64,1024]{2,0,1:T(1,128)S(1)}, u32[]{:S(2)}, u32[]{:S(2)}) async-start(f32[1,64,1024]{2,0,1:T(1,128)} %copy.126), calls=%async_computation.10 | async-start | bytes 524288 | tf_op jit(solution)/shard_map/all_to_all | solution.py:189
  473.5 39.6 %all_gather.3 = bf16[4096,64]{0,1:T(8,128)(2,1)S(1)} all-gather(bf16[128,64]{0,1:T(8,128)(2,1)S(1)} %fusion.8), channel_id=1, replica_groups=mesh['seq'=32,'grp'=16] {'seq'}, dimensions={0}, use_global_device_ids=true | all-gather | bytes 540672 | tf_op jit(solution)/shard_map/all_gather | solution.py:180
  515.2 25.0 %all-to-all-start.10 = ((f32[16,2,2,1024]{3,1,2,0:T(2,128)}), f32[16,2,2,1024]{3,1,2,0:T(2,128)S(1)}, u32[]{:S(2)}, u32[]{:S(2)}) async-start(f32[16,2,2,1024]{3,1,2,0:T(2,128)} %copy.128), calls=%async_computation.11 | async-start | bytes 524288 | tf_op jit(solution)/shard_map/all_to_all | solution.py:201
  543.5 8.4 %all-to-all-done.10 = f32[16,2,2,1024]{3,1,2,0:T(2,128)S(1)} async-done(((f32[16,2,2,1024]{3,1,2,0:T(2,128)}), f32[16,2,2,1024]{3,1,2,0:T(2,128)S(1)}, u32[]{:S(2)}, u32[]{:S(2)}) %all-to-all-start.10) | async-done | bytes 262176 | tf_op jit(solution)/shard_map/all_to_all | solution.py:201
  551.9 3.6 all-to-all-start.7
  556.7 26.0 %all-to-all-done.7 = f32[16,2,64,128]{3,1,2,0:T(2,128)S(1)} async-done(((f32[16,2,64,128]{3,1,2,0:T(2,128)}), f32[16,2,64,128]{3,1,2,0:T(2,128)S(1)}, u32[]{:S(2)}, u32[]{:S(2)}) %all-to-all-start.7) | async-done | bytes 1048608 | tf_op jit(solution)/shard_map/all_to_all | solution.py:194
  (131 shorter events, 74.1 us)
Async XLA Ops:
  7.2 28.3 %copy-start = (bf16[128,1024]{1,0:T(8,128)(2,1)S(1)}, bf16[128,1024]{1,0:T(8,128)(2,1)}, u32[]{:S(2)}) copy-start(bf16[128,1024]{1,0:T(8,128)(2,1)} %param.13) | copy-start | bytes 786436
  11.0 21.0 %all-to-all-start.4 = ((bf16[16,2,2,1024]{3,2,1,0:T(2,128)(2,1)}), bf16[16,2,2,1024]{3,2,1,0:T(2,128)(2,1)S(1)}, u32[]{:S(2)}, u32[]{:S(2)}) async-start(bf16[16,2,2,1024]{3,2,1,0:T(2,128)(2,1)} %copy.109), calls=%async_computation.4 | async-start | bytes 262144 | tf_op jit(solution)/shard_map/all_to_all | solution.py:104
  32.0 20.3 %all-to-all-start.8 = ((bf16[16,2,64,128]{3,2,1,0:T(8,128)(2,1)}), bf16[16,2,64,128]{3,2,1,0:T(8,128)(2,1)S(1)}, u32[]{:S(2)}, u32[]{:S(2)}) async-start(bf16[16,2,64,128]{3,2,1,0:T(8,128)(2,1)} %copy.122), calls=%async_computation.8 | async-start | bytes 1048576 | tf_op jit(solution)/shard_map/all_to_all | solution.py:103
  53.5 37.9 %all-to-all-start.1 = ((bf16[128,32,1,128]{3,0,2,1:T(8,128)(2,1)}), bf16[128,32,1,128]{3,0,2,1:T(8,128)(2,1)S(1)}, u32[]{:S(2)}, u32[]{:S(2)}) async-start(bf16[128,32,1,128]{3,0,2,1:T(8,128)(2,1)} %bitcast.10), calls=%async_computation.1 | async-start | bytes 2097152 | tf_op jit(solution)/shard_map/all_to_all | solution.py:153
  91.4 30.8 %all-to-all-start.2 = ((bf16[128,32,1,128]{3,0,2,1:T(8,128)(2,1)}), bf16[128,32,1,128]{3,0,2,1:T(8,128)(2,1)}, u32[]{:S(2)}, u32[]{:S(2)}) async-start(bf16[128,32,1,128]{3,0,2,1:T(8,128)(2,1)} %copy.104), calls=%async_computation.2 | async-start | bytes 2097152 | tf_op jit(solution)/shard_map/all_to_all | solution.py:154
  122.2 32.7 %all-to-all-start = ((bf16[128,32,1,128]{3,0,2,1:T(8,128)(2,1)}), bf16[128,32,1,128]{3,0,2,1:T(8,128)(2,1)}, u32[]{:S(2)}, u32[]{:S(2)}) async-start(bf16[128,32,1,128]{3,0,2,1:T(8,128)(2,1)} %copy.101), calls=%async_computation | async-start | bytes 2097152 | tf_op jit(solution)/shard_map/all_to_all | solution.py:152
  134.4 30.9 %copy-start.2 = (s32[32]{0:T(128)}, s32[32]{0:T(128)S(1)}, u32[]{:S(2)}) copy-start(s32[32]{0:T(128)S(1)} %select_reduce_fusion.1) | copy-start | bytes 388
  154.9 83.2 %all-to-all-start.6 = ((bf16[128,32,128]{2,0,1:T(8,128)(2,1)}), bf16[128,32,128]{2,0,1:T(8,128)(2,1)S(1)}, u32[]{:S(2)}, u32[]{:S(2)}) async-start(bf16[128,32,128]{2,0,1:T(8,128)(2,1)} %copy.113), calls=%async_computation.6 | async-start | bytes 2097152 | tf_op jit(solution)/shard_map/all_to_all | solution.py:131
  238.1 12.4 %copy-start.3 = (s32[32]{0:T(128)S(1)}, s32[32]{0:T(128)}, u32[]{:S(2)}) copy-start(s32[32]{0:T(128)} %copy-done.2) | copy-start | bytes 388
  238.1 33.8 %all-to-all-start.3 = ((bf16[32,2,8192]{2,1,0:T(2,128)(2,1)}), bf16[32,2,8192]{2,1,0:T(2,128)(2,1)S(1)}, u32[]{:S(2)}, u32[]{:S(2)}) async-start(bf16[32,2,8192]{2,1,0:T(2,128)(2,1)} %reshape.260), calls=%async_computation.3 | async-start | bytes 2097152 | tf_op jit(solution)/shard_map/all_to_all | solution.py:166
  247.4 217.5 %reduce-scatter.2.cloned.1.call-start = ((), (), s32[]{:S(2)}) async-start(), calls=%async_computation.12 | async-start | bytes 1081344 | tf_op jit(solution)/shard_map/reduce_scatter | solution.py:135
  271.9 1.0 copy-start.1
  272.9 193.9 %all-to-all-start.5 = ((bf16[32,2,1024]{2,1,0:T(2,128)(2,1)}), bf16[32,2,1024]{2,1,0:T(2,128)(2,1)S(1)}, u32[]{:S(2)}, u32[]{:S(2)}) async-start(bf16[32,2,1024]{2,1,0:T(2,128)(2,1)} %copy.111), calls=%async_computation.5 | async-start | bytes 262144 | tf_op jit(solution)/shard_map/all_to_all | solution.py:146
  286.7 227.2 %copy-start.4 = (s32[32]{0:T(128)S(1)}, s32[32]{0:T(128)}, u32[]{:S(2)}) copy-start(s32[32]{0:T(128)} %copy-done.2) | copy-start | bytes 388
  466.8 46.3 %all-to-all-start.9 = ((f32[1,64,1024]{2,0,1:T(1,128)}), f32[1,64,1024]{2,0,1:T(1,128)S(1)}, u32[]{:S(2)}, u32[]{:S(2)}) async-start(f32[1,64,1024]{2,0,1:T(1,128)} %copy.126), calls=%async_computation.10 | async-start | bytes 524288 | tf_op jit(solution)/shard_map/all_to_all | solution.py:189
  515.2 36.7 %all-to-all-start.10 = ((f32[16,2,2,1024]{3,1,2,0:T(2,128)}), f32[16,2,2,1024]{3,1,2,0:T(2,128)S(1)}, u32[]{:S(2)}, u32[]{:S(2)}) async-start(f32[16,2,2,1024]{3,1,2,0:T(2,128)} %copy.128), calls=%async_computation.11 | async-start | bytes 524288 | tf_op jit(solution)/shard_map/all_to_all | solution.py:201
  551.9 30.8 %all-to-all-start.7 = ((f32[16,2,64,128]{3,1,2,0:T(2,128)}), f32[16,2,64,128]{3,1,2,0:T(2,128)S(1)}, u32[]{:S(2)}, u32[]{:S(2)}) async-start(f32[16,2,64,128]{3,1,2,0:T(2,128)} %copy.117), calls=%async_computation.7 | async-start | bytes 2097152 | tf_op jit(solution)/shard_map/all_to_all | solution.py:194
Sparse Core Ops, SparseCore 0:
  252.6 212.2 reduce-scatter.1
where the time goes:
time: 594 us; the launch traced here: 592 us
  waiting for transfers between devices  322 us (54%)
  starting transfers between devices  100 us (17%)
  matrix products  60.2 us (10%)
  blocking collectives  39.6 us (7%)
  local copies, waits for them, and re-layouts  38.2 us (6%)
  between operations  14.4 us (2%)
  other arithmetic  12.6 us (2%)
    reduce_scatter x1, waiting for transfers between devices, local(): lax.psum_scatter(jnp.einsum('jyw,jaw->jya', token_rows, block_down_weight...  177 us
    all_gather x1, blocking collectives, local(): lax.all_gather(backward_rank_part.reshape(tokens_here, rank_overall), 'se...  39.6 us
    dot_general x8, matrix products, one_block(): jnp.dot(probabilities.T, grad_block, preferred_element_type=jnp.float32)  30.3 us
    all_to_all x1, waiting for transfers between devices, local(): lax.all_to_all(slot_down.reshape(group_count, capacity, rank_overall, por...  26 us
    all_to_all x1, waiting for transfers between devices, local(): lax.all_to_all(key_grid, 'seq', split_axis=1, concat_axis=0, tiled=True)  25.2 us
    all_to_all x1, starting transfers between devices, local(): lax.all_to_all(slot_up.reshape(group_count, capacity, rank_portion, value...  25 us
    all_to_all x1, waiting for transfers between devices, local(): lax.all_to_all(grad_grid, 'seq', split_axis=1, concat_axis=0, tiled=True)  22.2 us
    all_to_all x1, waiting for transfers between devices, local(): lax.all_to_all(head_grads, 'seq', split_axis=0, concat_axis=1, tiled=True)  20.3 us
  transfers between devices with their start and end apart: 12, of which 9 were waited for; matrix products, arithmetic and copies ran while one was open for 17% of the time, Pallas kernels for 0%

commit v1 on v0

--- a/solution.py
+++ b/solution.py
@@ -149,7 +149,9 @@
         frozen_key_rows.reshape(tokens_here, kv_heads, HEAD_DIM), group_size, axis=1
     ).reshape(tokens_here, shard_count, heads_here, HEAD_DIM)
     grad_grid = attention_output_gradient.reshape(tokens_here, shard_count, heads_here, HEAD_DIM)
-    query_all = lax.all_to_all(query_grid, "seq", split_axis=1, concat_axis=0, tiled=True)
+    query_all = jnp.concatenate(
+        lax.all_to_all(jnp.stack(jnp.split(query_grid, lax.axis_size("seq"), 1)), "seq", 0, 0), 0
+    )
     key_all = lax.all_to_all(key_grid, "seq", split_axis=1, concat_axis=0, tiled=True)
     grad_all = lax.all_to_all(grad_grid, "seq", split_axis=1, concat_axis=0, tiled=True)
 

time: 594 us -> 594 us (level)
    all_to_all x1, waiting for transfers between devices: 19.1 us -> 28.1 us  [local(): lax.all_to_all(jnp.stack(jnp.split(query_grid, lax.axis_size('seq'), 1)),...]
    unnamed x18 -> x51, local copies, waits for them, and re-layouts: 14.3 us -> 14.6 us
where the time goes in v1:
time: 594 us; the launch traced here: 592 us
  waiting for transfers between devices  321 us (54%)
  starting transfers between devices  100 us (17%)
  matrix products  60.1 us (10%)
  blocking collectives  39.6 us (7%)
  local copies, waits for them, and re-layouts  38.7 us (7%)
  between operations  14.5 us (2%)
  other arithmetic  12.6 us (2%)
    reduce_scatter x1, waiting for transfers between devices, local(): lax.psum_scatter(jnp.einsum('jyw,jaw->jya', token_rows, block_down_weight...  176 us
    all_gather x1, blocking collectives, local(): lax.all_gather(backward_rank_part.reshape(tokens_here, rank_overall), 'se...  39.6 us
    dot_general x8, matrix products, one_block(): jnp.dot(probabilities.T, grad_block, preferred_element_type=jnp.float32)  30.3 us
    all_to_all x1, waiting for transfers between devices, local(): lax.all_to_all(jnp.stack(jnp.split(query_grid, lax.axis_size('seq'), 1)),...  28.1 us
    all_to_all x1, waiting for transfers between devices, local(): lax.all_to_all(slot_down.reshape(group_count, capacity, rank_overall, por...  26 us
    all_to_all x1, starting transfers between devices, local(): lax.all_to_all(slot_up.reshape(group_count, capacity, rank_portion, value...  25 us
    all_to_all x1, waiting for transfers between devices, local(): lax.all_to_all(key_grid, 'seq', split_axis=1, concat_axis=0, tiled=True)  22.3 us
    all_to_all x1, waiting for transfers between devices, local(): lax.all_to_all(head_grads, 'seq', split_axis=0, concat_axis=1, tiled=True)  20.3 us
  transfers between devices with their start and end apart: 12, of which 9 were waited for; matrix products, arithmetic and copies ran while one was open for 17% of the time, Pallas kernels for 0%

profile of v1, /device:TPU:1, one launch (start us, length us, event | category | flops | bytes accessed | tf_op | source)
XLA Modules:
  0.0 591.8 jit_solution(13728101163112725445)
XLA Ops:
  11.0 11.8 %all-to-all-start.4 = ((bf16[16,2,2,1024]{3,2,1,0:T(2,128)(2,1)}), bf16[16,2,2,1024]{3,2,1,0:T(2,128)(2,1)S(1)}, u32[]{:S(2)}, u32[]{:S(2)}) async-start(bf16[16,2,2,1024]{3,2,1,0:T(2,128)(2,1)} %copy.233), calls=%async_computation.4 | async-start | bytes 262144 | tf_op jit(solution)/shard_map/all_to_all | solution.py:104
  27.0 5.0 all-to-all-done.4
  32.0 3.5 all-to-all-start.8
  36.8 15.5 %all-to-all-done.8 = bf16[16,2,64,128]{3,2,1,0:T(8,128)(2,1)S(1)} async-done(((bf16[16,2,64,128]{3,2,1,0:T(8,128)(2,1)}), bf16[16,2,64,128]{3,2,1,0:T(8,128)(2,1)S(1)}, u32[]{:S(2)}, u32[]{:S(2)}) %all-to-all-start.8) | async-done | bytes 524320 | tf_op jit(solution)/shard_map/all_to_all | solution.py:103
  52.3 9.7 %all-to-all-start = ((bf16[32,128,1,1,128]{4,1,3,2,0:T(8,128)(2,1)}), bf16[32,128,1,1,128]{4,1,3,2,0:T(8,128)(2,1)S(1)}, u32[]{:S(2)}, u32[]{:S(2)}) async-start(bf16[32,128,1,1,128]{4,1,3,2,0:T(8,128)(2,1)} %copy.225), calls=%async_computation | async-start | bytes 2097152 | tf_op jit(solution)/shard_map/all_to_all | solution.py:153
  62.1 28.1 %all-to-all-done = bf16[32,128,1,1,128]{4,1,3,2,0:T(8,128)(2,1)S(1)} async-done(((bf16[32,128,1,1,128]{4,1,3,2,0:T(8,128)(2,1)}), bf16[32,128,1,1,128]{4,1,3,2,0:T(8,128)(2,1)S(1)}, u32[]{:S(2)}, u32[]{:S(2)}) %all-to-all-start) | async-done | bytes 1048608 | tf_op jit(solution)/shard_map/all_to_all | solution.py:153
  91.6 5.4 all-to-all-start.1
  100.0 22.3 %all-to-all-done.1 = bf16[128,32,1,128]{3,0,2,1:T(8,128)(2,1)S(1)} async-done(((bf16[128,32,1,128]{3,0,2,1:T(8,128)(2,1)}), bf16[128,32,1,128]{3,0,2,1:T(8,128)(2,1)S(1)}, u32[]{:S(2)}, u32[]{:S(2)}) %all-to-all-start.1) | async-done | bytes 1048608 | tf_op jit(solution)/shard_map/all_to_all | solution.py:155
  122.2 8.1 %all-to-all-start.2 = ((bf16[128,32,1,128]{3,0,2,1:T(8,128)(2,1)}), bf16[128,32,1,128]{3,0,2,1:T(8,128)(2,1)}, u32[]{:S(2)}, u32[]{:S(2)}) async-start(bf16[128,32,1,128]{3,0,2,1:T(8,128)(2,1)} %copy.228), calls=%async_computation.2 | async-start | bytes 2097152 | tf_op jit(solution)/shard_map/all_to_all | solution.py:156
  135.8 19.1 %all-to-all-done.2 = bf16[128,32,1,128]{3,0,2,1:T(8,128)(2,1)} async-done(((bf16[128,32,1,128]{3,0,2,1:T(8,128)(2,1)}), bf16[128,32,1,128]{3,0,2,1:T(8,128)(2,1)}, u32[]{:S(2)}, u32[]{:S(2)}) %all-to-all-start.2) | async-done | bytes 1048608 | tf_op jit(solution)/shard_map/all_to_all | solution.py:156
  154.9 8.6 %all-to-all-start.6 = ((bf16[128,32,128]{2,0,1:T(8,128)(2,1)}), bf16[128,32,128]{2,0,1:T(8,128)(2,1)S(1)}, u32[]{:S(2)}, u32[]{:S(2)}) async-start(bf16[128,32,128]{2,0,1:T(8,128)(2,1)} %copy.237), calls=%async_computation.6 | async-start | bytes 2097152 | tf_op jit(solution)/shard_map/all_to_all | solution.py:131
  165.4 67.9 %while.19 = (s32[]{:T(128)}, f32[6144,128]{1,0:T(8,128)}, s32[8]{0:T(128)S(1)}, s32[6144]{0:T(1024)S(1)}, s32[4096]{0:T(1024)S(1)}, /*index=5*/bf16[4096,128]{1,...) while((s32[]{:T(128)}, f32[6144,128]{1,0:T(8,128)}, ...), condition=%wide.region_9.10_spmd, body=%wide.region_6.9_spmd.sunk | while | flops 685836288 | bytes 19343620 | solution.py:43
  170.1 3.8 fusion.64
  178.6 3.8 fusion.64
  187.0 3.8 fusion.64
  195.5 3.8 fusion.64
  204.1 3.8 fusion.64
  209.3 2.4 fusion.62
  212.6 3.8 fusion.64
  221.1 3.8 fusion.64
  229.6 3.8 fusion.64
  238.2 9.2 %all-to-all-start.3 = ((bf16[32,2,8192]{2,1,0:T(2,128)(2,1)}), bf16[32,2,8192]{2,1,0:T(2,128)(2,1)S(1)}, u32[]{:S(2)}, u32[]{:S(2)}) async-start(bf16[32,2,8192]{2,1,0:T(2,128)(2,1)} %reshape.259), calls=%async_computation.3 | async-start | bytes 2097152 | tf_op jit(solution)/shard_map/all_to_all | solution.py:168
  251.6 20.3 %all-to-all-done.3 = bf16[32,2,8192]{2,1,0:T(2,128)(2,1)S(1)} async-done(((bf16[32,2,8192]{2,1,0:T(2,128)(2,1)}), bf16[32,2,8192]{2,1,0:T(2,128)(2,1)S(1)}, u32[]{:S(2)}, u32[]{:S(2)}) %all-to-all-start.3) | async-done | bytes 1048608 | tf_op jit(solution)/shard_map/all_to_all | solution.py:168
  272.9 8.4 %all-to-all-start.5 = ((bf16[32,2,1024]{2,1,0:T(2,128)(2,1)}), bf16[32,2,1024]{2,1,0:T(2,128)(2,1)S(1)}, u32[]{:S(2)}, u32[]{:S(2)}) async-start(bf16[32,2,1024]{2,1,0:T(2,128)(2,1)} %copy.235), calls=%async_computation.5 | async-start | bytes 262144 | tf_op jit(solution)/shard_map/all_to_all | solution.py:146
  281.3 4.3 reshape.260
  288.4 176.3 %reduce-scatter.2.cloned.1.call-done = f32[128,64]{0,1:T(8,128)} async-done(((f32[4096,64]{0,1:T(8,128)}), f32[128,64]{0,1:T(8,128)}) %reduce-scatter.2.cloned.1.call-update) | async-done | bytes 32784 | tf_op jit(solution)/shard_map/reduce_scatter | solution.py:135
  466.6 6.7 %all-to-all-start.9 = ((f32[1,64,1024]{2,0,1:T(1,128)}), f32[1,64,1024]{2,0,1:T(1,128)S(1)}, u32[]{:S(2)}, u32[]{:S(2)}) async-start(f32[1,64,1024]{2,0,1:T(1,128)} %copy.250), calls=%async_computation.10 | async-start | bytes 524288 | tf_op jit(solution)/shard_map/all_to_all | solution.py:191
  473.6 39.6 %all_gather.3 = bf16[4096,64]{0,1:T(8,128)(2,1)S(1)} all-gather(bf16[128,64]{0,1:T(8,128)(2,1)S(1)} %fusion.8), channel_id=1, replica_groups=mesh['seq'=32,'grp'=16] {'seq'}, dimensions={0}, use_global_device_ids=true | all-gather | bytes 540672 | tf_op jit(solution)/shard_map/all_gather | solution.py:182
  515.2 25.0 %all-to-all-start.10 = ((f32[16,2,2,1024]{3,1,2,0:T(2,128)}), f32[16,2,2,1024]{3,1,2,0:T(2,128)S(1)}, u32[]{:S(2)}, u32[]{:S(2)}) async-start(f32[16,2,2,1024]{3,1,2,0:T(2,128)} %copy.252), calls=%async_computation.11 | async-start | bytes 524288 | tf_op jit(solution)/shard_map/all_to_all | solution.py:203
  543.5 8.4 %all-to-all-done.10 = f32[16,2,2,1024]{3,1,2,0:T(2,128)S(1)} async-done(((f32[16,2,2,1024]{3,1,2,0:T(2,128)}), f32[16,2,2,1024]{3,1,2,0:T(2,128)S(1)}, u32[]{:S(2)}, u32[]{:S(2)}) %all-to-all-start.10) | async-done | bytes 262176 | tf_op jit(solution)/shard_map/all_to_all | solution.py:203
  552.0 3.6 all-to-all-start.7
  556.8 26.0 %all-to-all-done.7 = f32[16,2,64,128]{3,1,2,0:T(2,128)S(1)} async-done(((f32[16,2,64,128]{3,1,2,0:T(2,128)}), f32[16,2,64,128]{3,1,2,0:T(2,128)S(1)}, u32[]{:S(2)}, u32[]{:S(2)}) %all-to-all-start.7) | async-done | bytes 1048608 | tf_op jit(solution)/shard_map/all_to_all | solution.py:196
  (165 shorter events, 74.5 us)
Async XLA Ops:
  7.2 54.8 %copy-start = (bf16[128,1024]{1,0:T(8,128)(2,1)S(1)}, bf16[128,1024]{1,0:T(8,128)(2,1)}, u32[]{:S(2)}) copy-start(bf16[128,1024]{1,0:T(8,128)(2,1)} %param.13) | copy-start | bytes 786436
  11.0 21.0 %all-to-all-start.4 = ((bf16[16,2,2,1024]{3,2,1,0:T(2,128)(2,1)}), bf16[16,2,2,1024]{3,2,1,0:T(2,128)(2,1)S(1)}, u32[]{:S(2)}, u32[]{:S(2)}) async-start(bf16[16,2,2,1024]{3,2,1,0:T(2,128)(2,1)} %copy.233), calls=%async_computation.4 | async-start | bytes 262144 | tf_op jit(solution)/shard_map/all_to_all | solution.py:104
  32.0 20.3 %all-to-all-start.8 = ((bf16[16,2,64,128]{3,2,1,0:T(8,128)(2,1)}), bf16[16,2,64,128]{3,2,1,0:T(8,128)(2,1)S(1)}, u32[]{:S(2)}, u32[]{:S(2)}) async-start(bf16[16,2,64,128]{3,2,1,0:T(8,128)(2,1)} %copy.246), calls=%async_computation.8 | async-start | bytes 1048576 | tf_op jit(solution)/shard_map/all_to_all | solution.py:103
  52.3 37.9 %all-to-all-start = ((bf16[32,128,1,1,128]{4,1,3,2,0:T(8,128)(2,1)}), bf16[32,128,1,1,128]{4,1,3,2,0:T(8,128)(2,1)S(1)}, u32[]{:S(2)}, u32[]{:S(2)}) async-start(bf16[32,128,1,1,128]{4,1,3,2,0:T(8,128)(2,1)} %copy.225), calls=%async_computation | async-start | bytes 2097152 | tf_op jit(solution)/shard_map/all_to_all | solution.py:153
  90.2 1.4 copy-start.2
  91.6 30.7 %all-to-all-start.1 = ((bf16[128,32,1,128]{3,0,2,1:T(8,128)(2,1)}), bf16[128,32,1,128]{3,0,2,1:T(8,128)(2,1)S(1)}, u32[]{:S(2)}, u32[]{:S(2)}) async-start(bf16[128,32,1,128]{3,0,2,1:T(8,128)(2,1)} %bitcast.71), calls=%async_computation.1 | async-start | bytes 2097152 | tf_op jit(solution)/shard_map/all_to_all | solution.py:155
  122.2 32.7 %all-to-all-start.2 = ((bf16[128,32,1,128]{3,0,2,1:T(8,128)(2,1)}), bf16[128,32,1,128]{3,0,2,1:T(8,128)(2,1)}, u32[]{:S(2)}, u32[]{:S(2)}) async-start(bf16[128,32,1,128]{3,0,2,1:T(8,128)(2,1)} %copy.228), calls=%async_computation.2 | async-start | bytes 2097152 | tf_op jit(solution)/shard_map/all_to_all | solution.py:156
  134.5 30.9 %copy-start.3 = (s32[32]{0:T(128)}, s32[32]{0:T(128)S(1)}, u32[]{:S(2)}) copy-start(s32[32]{0:T(128)S(1)} %select_reduce_fusion.1) | copy-start | bytes 388
  154.9 83.2 %all-to-all-start.6 = ((bf16[128,32,128]{2,0,1:T(8,128)(2,1)}), bf16[128,32,128]{2,0,1:T(8,128)(2,1)S(1)}, u32[]{:S(2)}, u32[]{:S(2)}) async-start(bf16[128,32,128]{2,0,1:T(8,128)(2,1)} %copy.237), calls=%async_computation.6 | async-start | bytes 2097152 | tf_op jit(solution)/shard_map/all_to_all | solution.py:131
  238.2 12.4 %copy-start.4 = (s32[32]{0:T(128)S(1)}, s32[32]{0:T(128)}, u32[]{:S(2)}) copy-start(s32[32]{0:T(128)} %copy-done.3) | copy-start | bytes 388
  238.2 33.7 %all-to-all-start.3 = ((bf16[32,2,8192]{2,1,0:T(2,128)(2,1)}), bf16[32,2,8192]{2,1,0:T(2,128)(2,1)S(1)}, u32[]{:S(2)}, u32[]{:S(2)}) async-start(bf16[32,2,8192]{2,1,0:T(2,128)(2,1)} %reshape.259), calls=%async_computation.3 | async-start | bytes 2097152 | tf_op jit(solution)/shard_map/all_to_all | solution.py:168
  247.4 217.3 %reduce-scatter.2.cloned.1.call-start = ((), (), s32[]{:S(2)}) async-start(), calls=%async_computation.12 | async-start | bytes 1081344 | tf_op jit(solution)/shard_map/reduce_scatter | solution.py:135
  271.9 1.0 copy-start.1
  272.9 193.7 %all-to-all-start.5 = ((bf16[32,2,1024]{2,1,0:T(2,128)(2,1)}), bf16[32,2,1024]{2,1,0:T(2,128)(2,1)S(1)}, u32[]{:S(2)}, u32[]{:S(2)}) async-start(bf16[32,2,1024]{2,1,0:T(2,128)(2,1)} %copy.235), calls=%async_computation.5 | async-start | bytes 262144 | tf_op jit(solution)/shard_map/all_to_all | solution.py:146
  286.8 227.2 %copy-start.5 = (s32[32]{0:T(128)S(1)}, s32[32]{0:T(128)}, u32[]{:S(2)}) copy-start(s32[32]{0:T(128)} %copy-done.3) | copy-start | bytes 388
  466.6 46.6 %all-to-all-start.9 = ((f32[1,64,1024]{2,0,1:T(1,128)}), f32[1,64,1024]{2,0,1:T(1,128)S(1)}, u32[]{:S(2)}, u32[]{:S(2)}) async-start(f32[1,64,1024]{2,0,1:T(1,128)} %copy.250), calls=%async_computation.10 | async-start | bytes 524288 | tf_op jit(solution)/shard_map/all_to_all | solution.py:191
  515.2 36.7 %all-to-all-start.10 = ((f32[16,2,2,1024]{3,1,2,0:T(2,128)}), f32[16,2,2,1024]{3,1,2,0:T(2,128)S(1)}, u32[]{:S(2)}, u32[]{:S(2)}) async-start(f32[16,2,2,1024]{3,1,2,0:T(2,128)} %copy.252), calls=%async_computation.11 | async-start | bytes 524288 | tf_op jit(solution)/shard_map/all_to_all | solution.py:203
  552.0 30.8 %all-to-all-start.7 = ((f32[16,2,64,128]{3,1,2,0:T(2,128)}), f32[16,2,64,128]{3,1,2,0:T(2,128)S(1)}, u32[]{:S(2)}, u32[]{:S(2)}) async-start(f32[16,2,64,128]{3,1,2,0:T(2,128)} %copy.241), calls=%async_computation.7 | async-start | bytes 2097152 | tf_op jit(solution)/shard_map/all_to_all | solution.py:196
Sparse Core Ops, SparseCore 0:
  252.6 212.0 reduce-scatter.1
